TPU v7x, 128 devices: a whole 4x4x4 slice. The times are simulated.
128 devices in a mesh: row: 16 (over z, x), col: 8 (over y, core).
Axes of the slice: x: 4, y: 4, z: 4, core: 2. Of those that a mesh axis runs over, the one named last changes fastest.
Arguments:
- child_front: bfloat16 [16, 4096, 1024], P('row', 'col'), may hold values from -6 to 6
- child_inverse: bfloat16 [16, 1024, 1024], P('row'), as said below
- child_index: int32 [16, 32], P('row'), may hold values from 0 to 79, as said below
- child_size: int32 [16], P('row'), may hold values from 4 to 32, as said below
- front: float32 [10240, 10240], P('row', 'col'), may hold values from -6 to 6
- panel_inverse: float32 [256, 256], replicated, as said below
Outputs:
- trailing: float32 [10240, 10240], P('row', 'col')
- panel_rows: float32 [10240, 256], P('row')
Inputs may be any that keep to these rules, and one draw needn't show every extreme that they name: `child_index`: for each child r, the entries t < child_size[r] are increasing root tile numbers; later entries are arbitrary tile numbers and are not used. Cutting the root tiles into aligned runs of 5 tiles, a child has at most 2 live tiles in any run, and exactly 2 in each of two neighbouring runs 2q and 2q + 1 for some q. `child_size`: some child has the smallest and some child the largest possible size in every draw. `child_inverse`: lower triangular with a positive diagonal. `panel_inverse`: lower triangular with a positive diagonal.
All inputs are finite; a program needn't handle non-finite values.
Results may differ from a plain program's by a relative error of at most 0.0034.
Values may be sent and summed in bfloat16 or wider, within the bound.
A program may use at most 128 MiB of HBM per device.

v0:
```python
import jax
import jax.numpy as jnp
from jax import lax
from jax.sharding import PartitionSpec as P

TILE = 128
PANEL = 256
BLOCK_TILES = 2


def from_root(value, axis, source):
    kept = jnp.where(lax.axis_index(axis) == source, value, 0).astype(value.dtype)
    return lax.psum(kept, axis)


def slot_tiles(tile_index, first_slot, slot_count, slot_width, base_tile, sentinel):
    positions = jnp.arange(slot_width, dtype=jnp.int32)
    picked = jnp.take(tile_index, jnp.clip(first_slot + positions, 0, tile_index.shape[0] - 1))
    return jnp.where(positions < slot_count, picked - base_tile, sentinel)


def shards(child_front, child_inverse, child_index, child_size, front, panel_inverse):
    precise = lax.Precision.HIGHEST
    rows_dev = front.shape[0]
    cols_dev = front.shape[1]
    tiles_row = rows_dev // TILE
    tiles_col = cols_dev // TILE
    blocks = lax.axis_size("row")
    column = lax.axis_index("col")
    double = 2 * BLOCK_TILES
    factor_part = lax.dot_general(
        child_front[0],
        child_inverse[0],
        (((1,), (1,)), ((), ())),
        preferred_element_type=jnp.float32,
    ).astype(jnp.bfloat16)
    factor = lax.all_gather(factor_part, "col", axis=0, tiled=True)
    tile_index = child_index[0]
    live_tiles = jnp.arange(tile_index.shape[0], dtype=jnp.int32) < child_size[0]
    row_owner = jnp.where(live_tiles, tile_index // tiles_row, blocks)
    targets = jnp.arange(blocks, dtype=jnp.int32)
    starts = jnp.sum((row_owner[None, :] < targets[:, None]).astype(jnp.int32), axis=1)
    counts = jnp.sum((row_owner[None, :] == targets[:, None]).astype(jnp.int32), axis=1)
    col_owner = jnp.where(live_tiles, tile_index // tiles_col, lax.axis_size("col"))
    col_start = jnp.sum((col_owner < column).astype(jnp.int32))
    col_count = jnp.sum((col_owner == column).astype(jnp.int32))
    padded = jnp.concatenate(
        [factor, jnp.zeros((double * TILE, factor.shape[1]), factor.dtype)], axis=0
    )

    def row_rows(first_tile):
        return lax.dynamic_slice_in_dim(padded, first_tile * TILE, BLOCK_TILES * TILE, 0)

    def row_slots(first_tile, tile_count, target):
        return slot_tiles(
            tile_index, first_tile, tile_count, BLOCK_TILES, target * tiles_row, tiles_row
        )

    row_parts = jax.vmap(row_rows)(starts)
    col_part = lax.dynamic_slice_in_dim(padded, col_start * TILE, double * TILE, 0)
    row_targets = jax.vmap(row_slots)(starts, counts, targets)
    col_targets = slot_tiles(
        tile_index, col_start, col_count, double, column * tiles_col, tiles_col
    )
    col_sent = jnp.broadcast_to(col_targets[None, :], (blocks, double))
    width = padded.shape[1]
    row_tiles = row_parts.reshape(blocks, BLOCK_TILES, TILE, width)
    col_tiles = col_part.reshape(double, TILE, width)
    contribution = -jnp.einsum(
        "ikap,jbp->ikjab", row_tiles, col_tiles, preferred_element_type=jnp.float32
    )
    arrived, arrived_rows, arrived_cols = (
        lax.all_to_all(contribution, "row", split_axis=0, concat_axis=0, tiled=True),
        lax.all_to_all(row_targets, "row", split_axis=0, concat_axis=0, tiled=True),
        lax.all_to_all(col_sent, "row", split_axis=0, concat_axis=0, tiled=True),
    )
    tiled = front.reshape(tiles_row, TILE, tiles_col, TILE)
    tiled = tiled.at[arrived_rows[:, :, None], :, arrived_cols[:, None, :], :].add(
        arrived, mode="drop"
    )
    assembled = tiled.reshape(rows_dev, cols_dev)
    own_panel = lax.dot_general(
        assembled[:, :PANEL], panel_inverse, (((1,), (1,)), ((), ())), precision=precise
    )
    panel_rows = from_root(own_panel, "col", 0)
    whole_panel = lax.all_gather(panel_rows, "row", axis=0, tiled=True)
    across = lax.dynamic_slice_in_dim(whole_panel, column * cols_dev, cols_dev, 0)
    trailing = assembled - lax.dot_general(
        panel_rows, across, (((1,), (1,)), ((), ())), precision=precise
    )
    return (trailing, panel_rows)


def solution(mesh):
    in_specs = (
        P("row", "col", None),
        P("row", None, None),
        P("row", None),
        P("row"),
        P("row", "col"),
        P(),
    )
    out_specs = (P("row", "col"), P("row", None))
    return jax.shard_map(shards, mesh=mesh, in_specs=in_specs, out_specs=out_specs, check_vma=False)
```

profile of v0, /device:TPU:20, one launch (start us, length us, event | category | flops | bytes accessed | tf_op | source)
XLA Modules:
  0.0 467.4 jit_solution(3586415045492164564)
XLA Ops:
  7.2 1.5 copy-done
  8.8 3.5 fusion.2
  13.2 0.7 gather_fusion
  14.0 0.7 subtract_select_fusion
  14.7 8.3 %all-to-all-start = ((s32[16,1,2]{2,1,0:T(1,128)}), s32[16,1,2]{2,1,0:T(1,128)S(1)}, u32[]{:S(2)}, u32[]{:S(2)}) async-start(s32[16,1,2]{2,1,0:T(1,128)} %bitcast.3), calls=%async_computation | async-start | bytes 16384 | tf_op jit(solution)/shard_map/all_to_all | solution.py:74
  23.0 0.7 fusion.12
  23.7 0.6 fusion.14
  24.4 0.6 gather_fusion.1
  25.7 1.3 compare_select_fusion.7
  27.0 36.2 %all-gather.3.cloned.1.call-done = bf16[4096,1024]{1,0:T(8,128)(2,1)} async-done(((bf16[512,1024]{1,0:T(8,128)(2,1)}), bf16[4096,1024]{1,0:T(8,128)(2,1)}) %all-gather.3.cloned.1.call-update) | async-done | bytes 8388624 | tf_op jit(solution)/shard_map/all_gather | solution.py:37
  63.2 8.0 %concatenate.10 = bf16[4608,1024]{1,0:T(8,128)(2,1)} pad(bf16[4096,1024]{1,0:T(8,128)(2,1)} %all-gather.3.cloned.1.call-done, bf16[]{:T(256)} %constant.41.clone.1), padding=0_512x0_0 | pad | bytes 17825794 | tf_op jit(solution)/shard_map/concatenate | solution.py:47
  71.3 51.5 %while.1 = (s32[]{:T(128)}, bf16[4608,1024]{1,0:T(8,128)(2,1)}, s32[16,2]{0,1:T(2,128)S(1)}, bf16[16,256,1024]{2,1,0:T(8,128)(2,1)}, s32[]{:T(128)}) while((s32[]{:T(128)}, bf16[4608,1024]{1,0:T(8,128)(2,1)}, s32[16,2]{0,1:T(2,128)S(1)}, bf16[16,256,1024]{2,1,0:T(8,128)(2,1)}, s32[]{:T(128)}) %tuple.22), condition=%wide.while_cond, body=%wide.while_body.sunk | while | flops 2 | bytes 1049689 | solution.py:52
  71.3 0.5 slice.25
  71.9 2.6 bitcast_dynamic-update-slice_fusion.2
  75.1 2.6 bitcast_dynamic-update-slice_fusion.2
  78.3 2.6 bitcast_dynamic-update-slice_fusion.2
  81.5 2.6 bitcast_dynamic-update-slice_fusion.2
  84.7 2.6 bitcast_dynamic-update-slice_fusion.2
  87.9 2.6 bitcast_dynamic-update-slice_fusion.2
  91.1 2.6 bitcast_dynamic-update-slice_fusion.2
  94.3 2.6 bitcast_dynamic-update-slice_fusion.2
  97.6 2.6 bitcast_dynamic-update-slice_fusion.2
  100.8 2.6 bitcast_dynamic-update-slice_fusion.2
  104.0 2.6 bitcast_dynamic-update-slice_fusion.2
  107.2 2.6 bitcast_dynamic-update-slice_fusion.2
  110.4 2.6 bitcast_dynamic-update-slice_fusion.2
  113.6 2.7 bitcast_dynamic-update-slice_fusion.2
  116.9 2.7 bitcast_dynamic-update-slice_fusion.2
  120.1 2.7 bitcast_dynamic-update-slice_fusion.2
  122.8 1.6 constant_dynamic-slice_fusion.1
  124.5 0.6 broadcast_in_dim.64
  125.1 7.3 %all-to-all-start.1 = ((s32[16,1,4]{2,1,0:T(1,128)}), s32[16,1,4]{2,1,0:T(1,128)S(1)}, u32[]{:S(2)}, u32[]{:S(2)}) async-start(s32[16,1,4]{2,1,0:T(1,128)} %broadcast_in_dim.64), calls=%async_computation.1 | async-start | bytes 16384 | tf_op jit(solution)/shard_map/all_to_all | solution.py:75
  132.4 7.0 %negate_bitcast_fusion = f32[16,2,4,128,128]{3,4,1,0,2:T(8,128)S(1)} fusion(bf16[4,128,1024,1,1]{2,1,4,3,0:T(8,128)(2,1)S(1)} %bitcast.66, bf16[16,2,128,1024,1]{3,2,1,0,4:T(8,128)(2,1)} %bitcast.67), kind=kOutput, calls=%fused_computation.5 | convolution fusion | flops 4297064448 | bytes 17825792 | tf_op jit(solution)/shard_map/ikap,jbp->ikjab/dot_general | solution.py:69
  139.4 3.8 copy.40
  143.2 7.5 %all-to-all-start.2 = ((f32[16,2,4,128,128]{3,4,1,2,0:T(8,128)}), f32[16,2,4,128,128]{3,4,1,2,0:T(8,128)}, u32[]{:S(2)}, u32[]{:S(2)}) async-start(f32[16,2,4,128,128]{3,4,1,2,0:T(8,128)} %copy.40), calls=%async_computation.2 | async-start | bytes 16777216 | tf_op jit(solution)/shard_map/all_to_all | solution.py:73
  150.9 2.9 reshape.279
  153.8 3.5 copy.42
  158.1 111.8 %all-to-all-done.2 = f32[16,2,4,128,128]{3,4,1,2,0:T(8,128)} async-done(((f32[16,2,4,128,128]{3,4,1,2,0:T(8,128)}), f32[16,2,4,128,128]{3,4,1,2,0:T(8,128)}, u32[]{:S(2)}, u32[]{:S(2)}) %all-to-all-start.2) | async-done | bytes 8388640 | tf_op jit(solution)/shard_map/all_to_all | solution.py:73
  269.9 9.2 %copy.41 = f32[16,2,4,128,128]{4,3,2,1,0:T(8,128)} copy(f32[16,2,4,128,128]{3,4,1,2,0:T(8,128)} %all-to-all-done.2) | data formatting | bytes 16777216 | tf_op jit(solution)/shard_map/all_to_all | solution.py:73
  279.2 19.2 %scatter_fusion = f32[5,128,10,128]{3,1,2,0:T(8,128)S(1)} fusion(f32[5,128,10,128]{3,1,2,0:T(8,128)S(1)} %copy.42, s32[128]{0:T(128)S(1)} %reshape.318, f32[128,128,128]{2,1,0:T(8,128)} %bitcast.62), kind=kCustom, calls=%fused_computation.2 | custom fusion | flops 2097152 | bytes 25166848 | tf_op jit(solution)/shard_map/scatter-add | solution.py:78
  298.4 2.0 copy.43
  300.3 1.6 copy.47
  302.0 1.7 copy-done.3
  303.7 1.6 convolution_select_fusion
  305.3 61.9 %all-reduce.4.cloned.1.call-done = f32[640,256]{1,0:T(8,128)} async-done(((f32[640,256]{1,0:T(8,128)}), f32[640,256]{1,0:T(8,128)}) %all-reduce.4.cloned.1.call-update) | async-done | bytes 655376 | tf_op jit(solution)/shard_map/psum | solution.py:13
  367.2 85.8 %all-gather.5.cloned.1.call-done = f32[10240,256]{1,0:T(8,128)} async-done(((f32[640,256]{1,0:T(8,128)}), f32[10240,256]{1,0:T(8,128)}) %all-gather.5.cloned.1.call-update) | async-done | bytes 10485776 | tf_op jit(solution)/shard_map/all_gather | solution.py:86
  453.0 7.0 %convolution_subtract_fusion = f32[640,1280]{1,0:T(8,128)} fusion(f32[640,1280]{1,0:T(8,128)} %bitcast.65, f32[640,256]{1,0:T(8,128)} %all-reduce.4.cloned.1.call-done, f32[10240,256]{1,0:T(8,128)} %all-gather.5.cloned.1.call-done, s32[]{:T(128)S(6)} %select_n.153), kind=kOutput, calls=%fused_computation.6 | convolution fusion | flops 2517401600 | bytes 8519684 | tf_op jit(solution)/shard_map/dot_general | solution.py:88
  460.0 0.8 copy.58
  (75 shorter events, 10.4 us)
Async XLA Ops:
  7.2 1.6 copy-start
  7.2 5.7 %copy-start.2 = (s32[1,32]{1,0:T(1,128)S(1)}, s32[1,32]{1,0:T(1,128)}, u32[]{:S(2)}) copy-start(s32[1,32]{1,0:T(1,128)} %param.8) | copy-start | bytes 388
  7.2 56.1 %all-gather.3.cloned.1.call-start = ((), (), s32[]{:S(2)}) async-start(), calls=%async_computation.3 | async-start | bytes 9437184 | tf_op jit(solution)/shard_map/all_gather | solution.py:37
  14.7 109.7 %all-to-all-start = ((s32[16,1,2]{2,1,0:T(1,128)}), s32[16,1,2]{2,1,0:T(1,128)S(1)}, u32[]{:S(2)}, u32[]{:S(2)}) async-start(s32[16,1,2]{2,1,0:T(1,128)} %bitcast.3), calls=%async_computation | async-start | bytes 16384 | tf_op jit(solution)/shard_map/all_to_all | solution.py:74
  125.1 18.1 %all-to-all-start.1 = ((s32[16,1,4]{2,1,0:T(1,128)}), s32[16,1,4]{2,1,0:T(1,128)S(1)}, u32[]{:S(2)}, u32[]{:S(2)}) async-start(s32[16,1,4]{2,1,0:T(1,128)} %broadcast_in_dim.64), calls=%async_computation.1 | async-start | bytes 16384 | tf_op jit(solution)/shard_map/all_to_all | solution.py:75
  143.2 7.7 %copy-start.5 = (f32[640,1280]{1,0:T(8,128)S(1)}, f32[640,1280]{1,0:T(8,128)}, u32[]{:S(2)}) copy-start(f32[640,1280]{1,0:T(8,128)} %param.10) | copy-start | bytes 9830404
  143.2 126.8 %all-to-all-start.2 = ((f32[16,2,4,128,128]{3,4,1,2,0:T(8,128)}), f32[16,2,4,128,128]{3,4,1,2,0:T(8,128)}, u32[]{:S(2)}, u32[]{:S(2)}) async-start(f32[16,2,4,128,128]{3,4,1,2,0:T(8,128)} %copy.40), calls=%async_computation.2 | async-start | bytes 16777216 | tf_op jit(solution)/shard_map/all_to_all | solution.py:73
  150.6 216.6 %all-reduce.4.cloned.1.call-start = ((), (), s32[]{:S(2)}) async-start(), calls=%async_computation.4 | async-start | bytes 1310720 | tf_op jit(solution)/shard_map/psum | solution.py:13
  298.4 5.3 %copy-start.6 = (f32[256,256]{1,0:T(8,128)S(1)}, f32[256,256]{1,0:T(8,128)}, u32[]{:S(2)}) copy-start(f32[256,256]{1,0:T(8,128)} %param.11) | copy-start | bytes 786436
  300.3 160.5 %copy-start.1 = (bf16[1,1024,1024]{2,1,0:T(8,128)(2,1)S(1)}, bf16[1,1024,1024]{2,1,0:T(8,128)(2,1)}, u32[]{:S(2)}) copy-start(bf16[1,1024,1024]{2,1,0:T(8,128)(2,1)} %param.7) | copy-start | bytes 6291460
  301.9 1.7 copy-start.3
  305.2 147.8 %all-gather.5.cloned.1.call-start = ((), (), s32[]{:S(2)}) async-start(), calls=%async_computation.5 | async-start | bytes 11141120 | tf_op jit(solution)/shard_map/all_gather | solution.py:86
  367.2 92.8 %copy-start.4 = (f32[640,256]{1,0:T(8,128)S(1)}, f32[640,256]{1,0:T(8,128)}, u32[]{:S(2)}) copy-start(f32[640,256]{1,0:T(8,128)} %all-reduce.4.cloned.1.call-done) | copy-start | bytes 1966084
Sparse Core Ops, SparseCore 0:
  12.4 50.8 all-gather.2
  305.4 61.7 all-reduce.3
  369.3 83.6 all-gather.4
where the time goes:
time: 470 us; the launch traced here: 467 us
  waiting for transfers between devices  296 us (63%)
  local copies, waits for them, and re-layouts  91 us (19%)
  starting transfers between devices  23.4 us (5%)
  other arithmetic  22.9 us (5%)
  matrix products  19 us (4%)
  between operations  15.3 us (3%)
    all_to_all x1, waiting for transfers between devices, shards(): lax.all_to_all(contribution, 'row', split_axis=0, concat_axis=0, tiled=True)  112 us
    all_gather x1, waiting for transfers between devices, shards(): whole_panel = lax.all_gather(panel_rows, 'row', axis=0, tiled=True)  85.8 us
    psum x1, waiting for transfers between devices, from_root(): return lax.psum(kept, axis)  61.9 us
    gather x48, local copies, waits for them, and re-layouts  51.5 us
    all_gather x1, waiting for transfers between devices, shards(): factor = lax.all_gather(factor_part, 'col', axis=0, tiled=True)  36.2 us
    scatter-add x1, other arithmetic, shards(): tiled.at[arrived_rows[:, :, None], :, arrived_cols[:, None, :], :]  19.2 us
  transfers between devices with their start and end apart: 6, of which 4 were waited for; matrix products, arithmetic and copies ran while one was open for 18% of the time, Pallas kernels for 0%

commit v1 on v0

v1 whole, which is shorter than its diff:
```python
import functools

import jax
import jax.numpy as jnp
from jax import lax
from jax.experimental import pallas as pl
from jax.experimental.pallas import tpu as pltpu
from jax.sharding import PartitionSpec as P

TILE = 128
PANEL = 256
RUN = 5
SLOTS = 32
PIV = 1024
RUNS = 16
COLS = 8
PART = 512
ROWS = RUN * TILE
PAIR = 2 * TILE
HALF = ROWS // 2
NT = (((1,), (1,)), ((), ()))
BF16 = jnp.bfloat16
F32 = jnp.float32


def tile_rows(index):
    return pl.ds(pl.multiple_of(index * TILE, TILE), TILE)


def exchange_kernel(
    meta_ref, meta_vmem, child_ref, inverse_ref, front_ref, panel_inverse_ref,
    arrived_first, arrived_second, panel_row, panel_col, meta_all,
    factor, column_tiles, outgoing, panel, meta_smem,
    own_send, pass_send, sibling_send, gather_recv,
    block_send, block_recv, meta_send, meta_recv, local_sem,
    row_send, row_recv, col_send, col_recv,
):
    arrived = (arrived_first, arrived_second)
    row = lax.axis_index("row")
    col = lax.axis_index("col")
    z, x = row // 4, row % 4
    y, core = col // 2, col % 2
    up = {"row": row, "col": ((y + 1) % 4) * 2 + core}
    down = {"row": row, "col": ((y + 3) % 4) * 2 + core}
    sibling = {"row": row, "col": y * 2 + 1 - core}

    def peer_row(step):
        return ((z + step // 4) % 4) * 4 + (x + step % 4) % 4

    def peer(step):
        return {"row": peer_row(step), "col": col}

    def remote(src, dst, send, recv, device):
        return pltpu.make_async_remote_copy(
            src_ref=src, dst_ref=dst, send_sem=send, recv_sem=recv,
            device_id=device, device_id_type=pl.DeviceIdType.MESH,
        )

    barrier = pltpu.get_barrier_semaphore()
    for device in (up, down, sibling):
        pl.semaphore_signal(barrier, inc=1, device_id=device, device_id_type=pl.DeviceIdType.MESH)

    @pl.loop(1, RUNS)
    def _(step):
        pl.semaphore_signal(barrier, inc=1, device_id=peer(step), device_id_type=pl.DeviceIdType.MESH)

    panel_in = pltpu.make_async_copy(front_ref.at[:, pl.ds(0, PANEL)], panel, local_sem.at[0])
    panel_in.start()

    def make_own(t):
        part = lax.dot_general(
            child_ref[0, pl.ds(t * TILE, TILE), :], inverse_ref[0], NT, preferred_element_type=F32
        )
        factor[col * 4 + t] = part.astype(BF16)

    for t in range(4):
        make_own(t)

    pl.semaphore_wait(barrier, 3 + RUNS - 1)

    @pl.loop(1, RUNS)
    def _(step):
        remote(meta_vmem, meta_all.at[row], meta_send.at[step], meta_recv.at[row], peer(step)).start()

    meta_own = pltpu.make_async_copy(meta_vmem, meta_all.at[row], local_sem.at[1])
    meta_own.start()

    def part_tile(c, t):
        return factor.at[c * 4 + t]

    def part_copy(c, t, send, device):
        return remote(part_tile(c, t), part_tile(c, t), send, gather_recv.at[c * 4 + t], device)

    below = ((y + 3) % 4) * 2 + core
    above = ((y + 1) % 4) * 2 + core
    across = ((y + 2) % 4) * 2 + core
    sent = []

    def send_part(c, t, send, device):
        copy = part_copy(c, t, send, device)
        copy.start()
        sent.append(copy)

    def recv_part(c, t):
        part_copy(c, t, own_send.at[0, 0], sibling).wait_recv()

    up_order, down_order = (0, 1, 2, 3), (2, 3, 0, 1)
    for a, b in zip(up_order, down_order):
        send_part(col, a, own_send.at[0, a], up)
        send_part(col, b, own_send.at[1, b], down)
    for t in range(4):
        send_part(col, t, sibling_send.at[0, t], sibling)
    for a, b in zip(up_order, down_order):
        recv_part(below, a)
        if a < 2:
            send_part(below, a, pass_send.at[0, a], up)
        send_part(below, a, sibling_send.at[1, a], sibling)
        recv_part(above, b)
        if b >= 2:
            send_part(above, b, pass_send.at[1, b - 2], down)
        send_part(above, b, sibling_send.at[2, b], sibling)
    for t in (0, 2, 1, 3):
        recv_part(across, t)
        send_part(across, t, sibling_send.at[3, t], sibling)
    for chip in range(4):
        for t in range(4):
            recv_part(chip * 2 + 1 - core, t)

    for slot in range(4):
        column_tiles[pl.ds(slot * TILE, TILE), :] = factor[meta_ref[0, col * 4 + slot]]

    def block(half, target):
        first = factor[meta_ref[0, 2 * target]]
        second = factor[meta_ref[0, 2 * target + 1]]
        rows = jnp.concatenate([first, second], axis=0)
        product = lax.dot_general(
            rows, column_tiles[pl.ds(half * PAIR, PAIR), :], NT, preferred_element_type=F32
        )
        return (-product).astype(BF16)

    def put_block(place, value):
        for a in range(2):
            for b in range(2):
                place[a, b] = value[a * TILE:(a + 1) * TILE, b * TILE:(b + 1) * TILE]

    def block_copy(half, step):
        return remote(
            outgoing.at[half, step], arrived[half].at[row],
            block_send.at[half, step], block_recv.at[half, row], peer(step),
        )

    for half in range(2):
        put_block(arrived[half].at[row], block(half, row))

        @pl.loop(1, RUNS)
        def _(step):
            put_block(outgoing.at[half, step], block(half, peer_row(step)))

            @pl.when(step > 1)
            def _():
                block_copy(half, step - 1).start()

        block_copy(half, RUNS - 1).start()

    def wait_blocks(half):
        @pl.loop(1, RUNS)
        def _(step):
            source = peer_row(step)
            remote(
                outgoing.at[half, step], arrived[half].at[source],
                block_send.at[half, step], block_recv.at[half, source], peer(step),
            ).wait_recv()

    meta_own.wait()

    @pl.loop(1, RUNS)
    def _(step):
        source = peer_row(step)
        remote(
            meta_vmem, meta_all.at[source], meta_send.at[step], meta_recv.at[source], peer(step)
        ).wait_recv()

    meta_in = pltpu.make_async_copy(meta_all, meta_smem, local_sem.at[2])
    meta_in.start()
    meta_in.wait()
    panel_in.wait()
    wait_blocks(0)

    def half_rows(h):
        return pl.ds(h * HALF, HALF)

    started = []

    def row_copy(h, kind, device):
        return remote(
            panel_row.at[half_rows(h), :], panel_row.at[half_rows(h), :],
            row_send.at[kind, h], row_recv.at[h], device,
        )

    def recv_row(h):
        row_copy(h, 0, sibling).wait_recv()

    @pl.when(col == 0)
    def _():
        @pl.loop(0, RUNS)
        def _(child):
            for i in range(RUN):
                row_slot = meta_smem[child, 2, RUN * row + i]
                row_here = meta_smem[child, 3, RUN * row + i]
                for j in range(PANEL // TILE):
                    col_slot = meta_smem[child, 2, j]
                    here = row_here * meta_smem[child, 3, j]
                    tile = arrived_first[child, row_slot, col_slot]
                    place = (pl.ds(i * TILE, TILE), pl.ds(j * TILE, TILE))
                    keep = jnp.full((TILE, TILE), here, jnp.int32) != 0
                    panel[place] += jnp.where(keep, tile.astype(F32), 0.0)

        panel_row[...] = lax.dot_general(
            panel[...], panel_inverse_ref[...], NT, precision=lax.Precision.HIGHEST,
            preferred_element_type=F32,
        ).astype(BF16)

    @pl.when(col == 0)
    def _():
        row_copy(0, 0, up).start()
        row_copy(1, 1, down).start()
        row_copy(1, 0, up).start()
        row_copy(0, 1, down).start()
        for h in range(2):
            row_copy(h, 2, sibling).start()

    @pl.when(col == 2)
    def _():
        recv_row(0)
        row_copy(0, 0, up).start()
        row_copy(0, 2, sibling).start()
        recv_row(1)
        row_copy(1, 2, sibling).start()

    @pl.when(col == 6)
    def _():
        recv_row(1)
        row_copy(1, 1, down).start()
        row_copy(1, 2, sibling).start()
        recv_row(0)
        row_copy(0, 2, sibling).start()

    @pl.when(col == 4)
    def _():
        recv_row(0)
        row_copy(0, 2, sibling).start()
        recv_row(1)
        row_copy(1, 2, sibling).start()

    @pl.when(core == 1)
    def _():
        recv_row(0)
        recv_row(1)

    kinds = (peer(4), peer(12), peer(1), peer(3))
    owner_dz = (z + 4 - y) % 4
    mine = (x // 2) == core

    def col_copy(j, h, kind):
        part = panel_col.at[j, half_rows(h), :]
        return remote(part, part, col_send.at[kind, h, j], col_recv.at[j, h], kinds[kind])

    def recv_col(j, h):
        col_copy(j, h, 0).wait_recv()

    @pl.when(mine & (owner_dz == 0))
    def _():
        panel_col[x % 2] = panel_row[...]
        col_copy(x % 2, 0, 0).start()
        col_copy(x % 2, 1, 1).start()
        col_copy(x % 2, 1, 0).start()
        col_copy(x % 2, 0, 1).start()
        col_copy(x % 2, 0, 2).start()
        col_copy(x % 2, 1, 3).start()
        col_copy(x % 2, 1, 2).start()
        col_copy(x % 2, 0, 3).start()

    @pl.when(mine & (owner_dz == 1))
    def _():
        recv_col(x % 2, 0)
        col_copy(x % 2, 0, 0).start()
        col_copy(x % 2, 0, 2).start()
        col_copy(x % 2, 0, 3).start()
        recv_col(x % 2, 1)
        col_copy(x % 2, 1, 2).start()
        col_copy(x % 2, 1, 3).start()

    @pl.when(mine & (owner_dz == 3))
    def _():
        recv_col(x % 2, 1)
        col_copy(x % 2, 1, 1).start()
        col_copy(x % 2, 1, 2).start()
        col_copy(x % 2, 1, 3).start()
        recv_col(x % 2, 0)
        col_copy(x % 2, 0, 2).start()
        col_copy(x % 2, 0, 3).start()

    @pl.when(mine & (owner_dz == 2))
    def _():
        recv_col(x % 2, 0)
        col_copy(x % 2, 0, 2).start()
        col_copy(x % 2, 0, 3).start()
        recv_col(x % 2, 1)
        col_copy(x % 2, 1, 2).start()
        col_copy(x % 2, 1, 3).start()

    for j in range(2):
        dx = (x + 4 - (2 * core + j)) % 4

        @pl.when(dx == 1)
        def _():
            recv_col(j, 0)
            col_copy(j, 0, 2).start()
            recv_col(j, 1)

        @pl.when(dx == 3)
        def _():
            recv_col(j, 1)
            col_copy(j, 1, 3).start()
            recv_col(j, 0)

        @pl.when(dx == 2)
        def _():
            recv_col(j, 0)
            recv_col(j, 1)

    wait_blocks(1)

    for copy in sent:
        copy.wait_send()
    for half in range(2):
        @pl.loop(1, RUNS)
        def _(step):
            block_copy(half, step).wait_send()

    @pl.loop(1, RUNS)
    def _(step):
        remote(meta_vmem, meta_all.at[row], meta_send.at[step], meta_recv.at[row], peer(step)).wait_send()

    for h in range(2):
        @pl.when(core == 0)
        def _():
            row_copy(h, 2, sibling).wait_send()

        @pl.when(col == 0)
        def _():
            row_copy(h, 0, up).wait_send()
            row_copy(h, 1, down).wait_send()

        for kind in (2, 3):
            @pl.when(mine)
            def _():
                col_copy(x % 2, h, kind).wait_send()

        @pl.when(mine & (owner_dz == 0))
        def _():
            col_copy(x % 2, h, 0).wait_send()
            col_copy(x % 2, h, 1).wait_send()

    @pl.when(col == 2)
    def _():
        row_copy(0, 0, up).wait_send()

    @pl.when(col == 6)
    def _():
        row_copy(1, 1, down).wait_send()

    @pl.when(mine & (owner_dz == 1))
    def _():
        col_copy(x % 2, 0, 0).wait_send()

    @pl.when(mine & (owner_dz == 3))
    def _():
        col_copy(x % 2, 1, 1).wait_send()

    for j in range(2):
        dx = (x + 4 - (2 * core + j)) % 4

        @pl.when(dx == 1)
        def _():
            col_copy(j, 0, 2).wait_send()

        @pl.when(dx == 3)
        def _():
            col_copy(j, 1, 3).wait_send()


def exchange(meta, child_front, child_inverse, front, panel_inverse):
    vmem = pl.BlockSpec(memory_space=pltpu.VMEM)
    dma = pltpu.SemaphoreType.DMA
    return pl.pallas_call(
        exchange_kernel,
        out_shape=(
            jax.ShapeDtypeStruct((RUNS, 2, 2, TILE, TILE), BF16),
            jax.ShapeDtypeStruct((RUNS, 2, 2, TILE, TILE), BF16),
            jax.ShapeDtypeStruct((ROWS, PANEL), BF16),
            jax.ShapeDtypeStruct((2, ROWS, PANEL), BF16),
            jax.ShapeDtypeStruct((RUNS, 8, 128), jnp.int32),
        ),
        in_specs=[
            pl.BlockSpec(memory_space=pltpu.SMEM), vmem, vmem, vmem,
            pl.BlockSpec(memory_space=pl.ANY), vmem,
        ],
        out_specs=(vmem, vmem, vmem, vmem, vmem),
        scratch_shapes=[
            pltpu.VMEM((SLOTS, TILE, PIV), BF16),
            pltpu.VMEM((4 * TILE, PIV), BF16),
            pltpu.VMEM((2, RUNS, 2, 2, TILE, TILE), BF16),
            pltpu.VMEM((ROWS, PANEL), F32),
            pltpu.SMEM((RUNS, 8, 128), jnp.int32),
            dma((2, 4)), dma((2, 2)), dma((4, 4)), dma((SLOTS,)),
            dma((2, RUNS)), dma((2, RUNS)), dma((RUNS,)), dma((RUNS,)), dma((3,)),
            dma((3, 2)), dma((2,)), dma((4, 2, 2)), dma((2, 2)),
        ],
        compiler_params=pltpu.CompilerParams(
            collective_id=0, has_side_effects=True, vmem_limit_bytes=56 << 20
        ),
        name="exchange",
    )(meta, meta, child_front, child_inverse, front, panel_inverse)


def finish_kernel(meta_ref, front_ref, arrived_first, arrived_second, panel_row, panel_col, trailing):
    row = lax.axis_index("row")
    col = lax.axis_index("col")
    rows = panel_row[...]
    for half in range(2):
        span = pl.ds(half * ROWS, ROWS)
        trailing[:, span] = front_ref[:, span] - lax.dot_general(
            rows, panel_col[half], NT, preferred_element_type=F32
        )
    for half in range(2):
        @pl.loop(0, RUNS)
        def _(child):
            for a in range(2):
                tile_row = meta_ref[child, 1, 2 * row + a]
                for b in range(2):
                    tile_col = meta_ref[child, 1, 4 * col + 2 * half + b]

                    @pl.when((tile_row >= 0) & (tile_col >= 0))
                    def _():
                        place = (tile_rows(tile_row), tile_rows(half * RUN + tile_col))
                        tile = (arrived_first, arrived_second)[half][child, a, b]
                        trailing[place] += tile.astype(F32)


def finish(meta_all, front, arrived_first, arrived_second, panel_row, panel_col):
    vmem = pl.BlockSpec(memory_space=pltpu.VMEM)
    return pl.pallas_call(
        finish_kernel,
        out_shape=jax.ShapeDtypeStruct(front.shape, F32),
        in_specs=[pl.BlockSpec(memory_space=pltpu.SMEM), vmem, vmem, vmem, vmem, vmem],
        out_specs=vmem,
        compiler_params=pltpu.CompilerParams(vmem_limit_bytes=40 << 20),
        name="finish",
    )(meta_all, front, arrived_first, arrived_second, panel_row, panel_col)


def slot_table(child_index, child_size):
    places = jnp.arange(SLOTS, dtype=jnp.int32)
    tiles = jnp.where(places < child_size[0], child_index[0], RUN * RUNS)
    before = jnp.sum((tiles[None, :] < RUN * (places // 2)[:, None]).astype(jnp.int32), axis=1)
    place = jnp.minimum(before + places % 2, SLOTS - 1)
    picked = jnp.sum(jnp.where(place[:, None] == places[None, :], tiles[None, :], 0), axis=1)
    local = picked - RUN * (places // 2)
    live = (local >= 0) & (local < RUN) & (before + places % 2 < SLOTS)
    wanted = jnp.arange(RUN * RUNS, dtype=jnp.int32)
    match = (picked[None, :] == wanted[:, None]) & live[None, :]
    slot = jnp.sum(jnp.where(match, places % 2, 0), axis=1)
    held = jnp.sum(match.astype(jnp.int32), axis=1)

    def lane(values):
        return jnp.pad(values, (0, 128 - values.shape[0]))

    table = jnp.stack([lane(place), lane(jnp.where(live, local, -1)), lane(slot), lane(held)])
    return jnp.pad(table, ((0, 4), (0, 0)))


def shards(child_front, child_inverse, child_index, child_size, front, panel_inverse):
    meta = slot_table(child_index, child_size)
    arrived_first, arrived_second, panel_row, panel_col, meta_all = exchange(
        meta, child_front, child_inverse, front, panel_inverse
    )
    trailing = finish(meta_all, front, arrived_first, arrived_second, panel_row, panel_col)
    return trailing, panel_row.astype(F32)


def solution(mesh):
    in_specs = (
        P("row", "col", None),
        P("row", None, None),
        P("row", None),
        P("row"),
        P("row", "col"),
        P(),
    )
    out_specs = (P("row", "col"), P("row", None))
    return jax.shard_map(shards, mesh=mesh, in_specs=in_specs, out_specs=out_specs, check_vma=False)
```

time: 470 us -> 141 us (0.30)
  the two profiles are of different devices: /device:TPU:20 before, /device:TPU:110 now
where the time goes in v1:
time: 141 us
  Pallas kernels  131 us (93%)
  local copies, waits for them, and re-layouts  6.68 us (5%)
  other arithmetic  2.04 us (1%)
    pallas_call x1, Pallas kernels, exchange(): pl.pallas_call(exchange_kernel, out_shape=(jax.ShapeDtypeStruct((RUNS, 2,...  125 us
    pallas_call x1, Pallas kernels, finish(): pl.pallas_call(finish_kernel, out_shape=jax.ShapeDtypeStruct(front.shape,...  6.11 us
    unnamed x12, local copies, waits for them, and re-layouts  6.08 us

profile of v1, /device:TPU:110, one launch (start us, length us, event | category | flops | bytes accessed | tf_op | source)
XLA Modules:
  0.0 141.0 jit_solution(15764958901423358612)
XLA Ops:
  1.3 0.7 fusion.2
  1.9 0.2 convert_reduce_fusion.1
  2.1 0.2 select_reduce_fusion.1
  2.4 0.1 select_reduce_fusion
  2.5 0.6 pad.22.meta_ref.meta_vmem
  3.1 0.0 copy-start
  3.1 124.8 %exchange.1 = (bf16[16,2,2,128,128]{4,3,2,1,0:T(8,128)(2,1)}, bf16[16,2,2,128,128]{4,3,2,1,0:T(8,128)(2,1)}, bf16[640,256]{1,0:T(8,128)(2,1)}, bf16[2,640,256]{2,1,0:T(8,128)(2,1)}, s32[16,8,128]{2,1,0:T(8,128)}) custom-call(s32[8,128]{1,0:T(8,128)} %pad.22.meta_ref.meta_vmem, s32[8,128]{1,0:T(8,128)} %pad.22.meta_ref.meta_vmem, ...), custom_call_target="tpu_custom_call" | custom-call | tf_op jit(solution)/shard_map/exchange/pallas_call | solution.py:396
  127.9 0.0 copy-done
  127.9 0.0 copy-start.1
  127.9 1.6 %copy-done.1 = bf16[16,2,2,128,128]{4,3,2,1,0:T(8,128)(2,1)S(1)} copy-done((bf16[16,2,2,128,128]{4,3,2,1,0:T(8,128)(2,1)S(1)}, bf16[16,2,2,128,128]{4,3,2,1,0:T(8,128)(2,1)}, u32[]{:S(2)}) %copy-start.1) | copy-done | bytes 2097176
  129.5 0.0 copy-start.2
  129.5 1.6 %copy-done.2 = bf16[16,2,2,128,128]{4,3,2,1,0:T(8,128)(2,1)S(1)} copy-done((bf16[16,2,2,128,128]{4,3,2,1,0:T(8,128)(2,1)S(1)}, bf16[16,2,2,128,128]{4,3,2,1,0:T(8,128)(2,1)}, u32[]{:S(2)}) %copy-start.2) | copy-done | bytes 2097176
  131.1 0.0 copy-start.3
  131.1 1.0 copy-done.3
  132.1 0.0 copy-start.4
  132.1 1.1 copy-done.4
  133.2 0.0 copy-start.5
  133.2 0.8 copy-done.5
  134.0 6.1 %finish.1 = f32[640,1280]{1,0:T(8,128)} custom-call(s32[16,8,128]{2,1,0:T(8,128)S(1)} %copy-done.5, f32[640,1280]{1,0:T(8,128)S(1)} %copy-done, bf16[16,2,2,128,128]{4,3,2,1,0:T(8,128)(2,1)S(1)} %copy-done.1, bf16[16,2,2,128,128]{4,3,2,1,0:T(8,128)(2,1)S(1)} %copy-done.2, bf16[640,256]{1,0:T(8,128)(2,1)S(1)} %copy-done.3, bf16[2,640,256]{2,1,0:T(8,128)(2,1)S(1)} %copy-done.4), custom_call_target="tpu_custom_call" | custom-call | tf_op jit(solution)/shard_map/finish/pallas_call | solution.py:453
  140.1 0.9 convert_element_type.11
  (7 shorter events, 0.0 us)
Async XLA Ops:
  3.1 124.8 %copy-start = (f32[640,1280]{1,0:T(8,128)S(1)}, f32[640,1280]{1,0:T(8,128)}, u32[]{:S(2)}) copy-start(f32[640,1280]{1,0:T(8,128)} %front_ref.3) | copy-start | bytes 9830404
  127.9 1.6 %copy-start.1 = (bf16[16,2,2,128,128]{4,3,2,1,0:T(8,128)(2,1)S(1)}, bf16[16,2,2,128,128]{4,3,2,1,0:T(8,128)(2,1)}, u32[]{:S(2)}) copy-start(bf16[16,2,2,128,128]{4,3,2,1,0:T(8,128)(2,1)} %get-tuple-element.8.arrived_first) | copy-start | bytes 6291460
  129.5 1.6 %copy-start.2 = (bf16[16,2,2,128,128]{4,3,2,1,0:T(8,128)(2,1)S(1)}, bf16[16,2,2,128,128]{4,3,2,1,0:T(8,128)(2,1)}, u32[]{:S(2)}) copy-start(bf16[16,2,2,128,128]{4,3,2,1,0:T(8,128)(2,1)} %get-tuple-element.9.arrived_second) | copy-start | bytes 6291460
  131.1 1.0 copy-start.3
  132.1 1.1 copy-start.4
  133.2 0.8 copy-start.5

commit v2 on v1

v2 whole, which is shorter than its diff:
```python
import functools

import jax
import jax.numpy as jnp
from jax import lax
from jax.experimental import pallas as pl
from jax.experimental.pallas import tpu as pltpu
from jax.sharding import PartitionSpec as P

TILE = 128
PANEL = 256
RUN = 5
SLOTS = 32
PIV = 1024
RUNS = 16
COLS = 8
PART = 512
ROWS = RUN * TILE
PAIR = 2 * TILE
HALF = ROWS // 2
NT = (((1,), (1,)), ((), ()))
NEAR = (1, 3, 4, 12, 5, 15, 7, 13, 2, 8, 9, 6, 11, 14, 10)
EARLY, MIDDLE = 4, 9
BF16 = jnp.bfloat16
F32 = jnp.float32


def tile_rows(index):
    return pl.ds(pl.multiple_of(index * TILE, TILE), TILE)


def exchange_kernel(
    meta_ref, meta_vmem, child_ref, inverse_hbm, front_ref, panel_inverse_ref,
    arrived_first, arrived_second, panel_row, work, meta_all,
    children, factor, column_tiles, outgoing, panel, panel_col, inverse_ref, meta_smem,
    own_send, pass_send, sibling_send, gather_recv,
    block_send, block_recv, meta_send, meta_recv, local_sem,
    row_send, row_recv, col_send, col_recv,
):
    arrived = (arrived_first, arrived_second)
    row = lax.axis_index("row")
    col = lax.axis_index("col")
    z, x = row // 4, row % 4
    y, core = col // 2, col % 2
    up = {"row": row, "col": ((y + 1) % 4) * 2 + core}
    down = {"row": row, "col": ((y + 3) % 4) * 2 + core}
    sibling = {"row": row, "col": y * 2 + 1 - core}

    def peer_row(step):
        return ((z + step // 4) % 4) * 4 + (x + step % 4) % 4

    def peer(step):
        return {"row": peer_row(step), "col": col}

    def remote(src, dst, send, recv, device):
        return pltpu.make_async_remote_copy(
            src_ref=src, dst_ref=dst, send_sem=send, recv_sem=recv,
            device_id=device, device_id_type=pl.DeviceIdType.MESH,
        )

    barrier = pltpu.get_barrier_semaphore()
    for device in (up, down, sibling):
        pl.semaphore_signal(barrier, inc=1, device_id=device, device_id_type=pl.DeviceIdType.MESH)

    @pl.loop(1, RUNS)
    def _(step):
        pl.semaphore_signal(barrier, inc=1, device_id=peer(step), device_id_type=pl.DeviceIdType.MESH)

    inverse_in = pltpu.make_async_copy(inverse_hbm.at[0], inverse_ref, local_sem.at[2])
    inverse_in.start()
    child_in = pltpu.make_async_copy(child_ref.at[0], children.at[pl.ds(col * 4, 4)], local_sem.at[3])
    child_in.start()
    front_in = pltpu.make_async_copy(front_ref, work, local_sem.at[0])
    front_in.start()
    pl.semaphore_wait(barrier, 3 + RUNS - 1)

    def part_copy(c, t, send, device):
        tile = children.at[c * 4 + t]
        return remote(tile, tile, send, gather_recv.at[c * 4 + t], device)

    below = ((y + 3) % 4) * 2 + core
    above = ((y + 1) % 4) * 2 + core
    across = ((y + 2) % 4) * 2 + core
    sent = []

    def send_part(c, t, send, device, own=False):
        copy = part_copy(c, t, send, device)
        if own:
            copy = remote(
                child_ref.at[0, t], children.at[c * 4 + t], send, gather_recv.at[c * 4 + t], device
            )
        copy.start()
        sent.append(copy)

    def recv_part(c, t):
        part_copy(c, t, own_send.at[0, 0], sibling).wait_recv()

    def make_factor(*tiles):
        rows = jnp.concatenate([children[c * 4 + t] for c, t in tiles], axis=0)
        for j in range(PIV // PAIR):
            depth = (j + 1) * PAIR
            part = lax.dot_general(
                rows[:, :depth], inverse_ref[pl.ds(j * PAIR, PAIR), pl.ds(0, depth)], NT,
                preferred_element_type=F32,
            ).astype(BF16)
            for i, (c, t) in enumerate(tiles):
                factor[c * 4 + t, :, pl.ds(j * PAIR, PAIR)] = part[i * TILE:(i + 1) * TILE]

    up_order, down_order = (0, 1, 2, 3), (2, 3, 0, 1)
    for a, b in zip(up_order, down_order):
        send_part(col, a, own_send.at[0, a], up, own=True)
        send_part(col, b, own_send.at[1, b], down, own=True)
    for t in range(4):
        send_part(col, t, sibling_send.at[0, t], sibling, own=True)

    @pl.loop(1, RUNS)
    def _(step):
        remote(meta_vmem, meta_all.at[row], meta_send.at[step], meta_recv.at[row], peer(step)).start()

    meta_own = pltpu.make_async_copy(meta_vmem, meta_all.at[row], local_sem.at[1])
    meta_own.start()
    child_in.wait()
    inverse_in.wait()
    make_factor((col, 0), (col, 1), (col, 2), (col, 3))
    partner = y * 2 + 1 - core
    for t in range(4):
        recv_part(partner, t)
    make_factor((partner, 0), (partner, 1), (partner, 2), (partner, 3))
    twins = tuple(((y + d) % 4) * 2 + 1 - core for d in (3, 1, 2))
    for a, b in zip(up_order, down_order):
        recv_part(below, a)
        if a < 2:
            send_part(below, a, pass_send.at[0, a], up)
        send_part(below, a, sibling_send.at[1, a], sibling)
        recv_part(above, b)
        if b >= 2:
            send_part(above, b, pass_send.at[1, b - 2], down)
        send_part(above, b, sibling_send.at[2, b], sibling)
        make_factor((below, a), (above, b))
        recv_part(twins[0], a)
        recv_part(twins[1], b)
        make_factor((twins[0], a), (twins[1], b))
    for a, b in ((0, 2), (1, 3)):
        for t in (a, b):
            recv_part(across, t)
            send_part(across, t, sibling_send.at[3, t], sibling)
        make_factor((across, a), (across, b))
        for t in (a, b):
            recv_part(twins[2], t)
        make_factor((twins[2], a), (twins[2], b))

    meta_own.wait()

    @pl.loop(1, RUNS)
    def _(step):
        source = peer_row(step)
        remote(
            meta_vmem, meta_all.at[source], meta_send.at[step], meta_recv.at[source], peer(step)
        ).wait_recv()

    meta_in = pltpu.make_async_copy(meta_all, meta_smem, local_sem.at[1])
    meta_in.start()

    for slot in range(4):
        column_tiles[pl.ds(slot * TILE, TILE), :] = factor[meta_ref[0, col * 4 + slot]]

    def block(half, target):
        first = factor[meta_ref[0, 2 * target]]
        second = factor[meta_ref[0, 2 * target + 1]]
        rows = jnp.concatenate([first, second], axis=0)
        product = lax.dot_general(
            rows, column_tiles[pl.ds(half * PAIR, PAIR), :], NT, preferred_element_type=F32
        )
        return (-product).astype(BF16)

    def put_block(place, value):
        for a in range(2):
            for b in range(2):
                place[a, b] = value[a * TILE:(a + 1) * TILE, b * TILE:(b + 1) * TILE]

    def block_copy(half, step):
        return remote(
            outgoing.at[half, step], arrived[half].at[row],
            block_send.at[half, step], block_recv.at[half, row], peer(step),
        )

    eager = col != 1
    for half in range(2):
        put_block(arrived[half].at[row], block(half, row))
        held = None
        for step in NEAR:
            put_block(outgoing.at[half, step], block(half, peer_row(step)))
            if held is not None:
                @pl.when(eager)
                def _():
                    block_copy(half, held).start()
            held = step if half == 0 or step in NEAR[:EARLY] else None
        if held is not None:
            @pl.when(eager)
            def _():
                block_copy(half, held).start()

    @pl.when(col == 1)
    def _():
        for half in range(2):
            for step in NEAR if half == 0 else NEAR[:EARLY]:
                block_copy(half, step).start()

    def send_late(first, last):
        for step in NEAR[first:last]:
            block_copy(1, step).start()

    def wait_blocks(half):
        @pl.loop(1, RUNS)
        def _(step):
            source = peer_row(step)
            remote(
                outgoing.at[half, step], arrived[half].at[source],
                block_send.at[half, step], block_recv.at[half, source], peer(step),
            ).wait_recv()

    meta_in.wait()
    front_in.wait()
    wait_blocks(0)

    def half_rows(h):
        return pl.ds(h * HALF, HALF)

    def row_copy(h, kind, device):
        return remote(
            panel_row.at[half_rows(h), :], panel_row.at[half_rows(h), :],
            row_send.at[kind, h], row_recv.at[h], device,
        )

    def recv_row(h):
        row_copy(h, 0, sibling).wait_recv()

    @pl.when(col == 0)
    def _():
        for j in range(PANEL // TILE):
            @pl.loop(0, RUN)
            def _(i):
                def add(child, total):
                    tile = arrived_first[
                        child, meta_smem[child, 2, RUN * row + i], meta_smem[child, 2, j]
                    ]
                    here = meta_smem[child, 3, RUN * row + i] * meta_smem[child, 3, j]
                    keep = jnp.full((TILE, TILE), here, jnp.int32) != 0
                    return total + jnp.where(keep, tile.astype(F32), 0.0)

                start = work[tile_rows(i), pl.ds(j * TILE, TILE)]
                panel[tile_rows(i), pl.ds(j * TILE, TILE)] = lax.fori_loop(0, RUNS, add, start, unroll=4)

        for h in range(2):
            panel_row[half_rows(h), :] = lax.dot_general(
                panel[half_rows(h), :], panel_inverse_ref[...], NT, precision=lax.Precision.HIGHEST,
                preferred_element_type=F32,
            ).astype(BF16)

    kinds = (peer(4), peer(12), peer(1), peer(3))
    owner_dz = (z + 4 - y) % 4
    mine = (x // 2) == core

    def col_copy(j, h, kind):
        part = panel_col.at[j, half_rows(h), :]
        return remote(part, part, col_send.at[kind, h, j], col_recv.at[j, h], kinds[kind])

    def source_copy(h, kind):
        return remote(
            panel_row.at[half_rows(h), :], panel_col.at[x % 2, half_rows(h), :],
            col_send.at[kind, h, x % 2], col_recv.at[x % 2, h], kinds[kind],
        )

    def recv_col(j, h):
        col_copy(j, h, 0).wait_recv()

    def row_stage(h):
        @pl.when(col == 0)
        def _():
            row_copy(h, 0, up).start()
            row_copy(h, 1, down).start()

        @pl.when((core == 1) | (y > 0))
        def _():
            recv_row(h)

        if h == 0:
            @pl.when(col == 2)
            def _():
                row_copy(h, 0, up).start()
        else:
            @pl.when(col == 6)
            def _():
                row_copy(h, 1, down).start()

        @pl.when(core == 0)
        def _():
            row_copy(h, 2, sibling).start()

        @pl.when(mine & (owner_dz == 0))
        def _():
            for kind in range(4):
                source_copy(h, kind).start()
            panel_col[x % 2, half_rows(h), :] = panel_row[half_rows(h), :]

    def z_stage(h):
        @pl.when(mine & (owner_dz != 0))
        def _():
            recv_col(x % 2, h)
            if h == 0:
                @pl.when(owner_dz == 1)
                def _():
                    col_copy(x % 2, h, 0).start()
            else:
                @pl.when(owner_dz == 3)
                def _():
                    col_copy(x % 2, h, 1).start()
            col_copy(x % 2, h, 2).start()
            col_copy(x % 2, h, 3).start()

    def x_stage(h):
        for j in range(2):
            dx = (x + 4 - (2 * core + j)) % 4

            @pl.when(dx != 0)
            def _():
                recv_col(j, h)

            @pl.when(dx == (1 if h == 0 else 3))
            def _():
                col_copy(j, h, 2 if h == 0 else 3).start()

    row_stage(0)
    row_stage(1)
    send_late(EARLY, MIDDLE)
    z_stage(0)
    z_stage(1)
    send_late(MIDDLE, RUNS - 1)
    x_stage(0)
    x_stage(1)

    for half in range(2):
        span = pl.ds(half * ROWS, ROWS)
        work[:, span] -= lax.dot_general(
            panel_row[...], panel_col[half], NT, preferred_element_type=F32
        )
    wait_blocks(1)

    for copy in sent:
        copy.wait_send()
    for half in range(2):
        @pl.loop(1, RUNS)
        def _(step):
            block_copy(half, step).wait_send()

    @pl.loop(1, RUNS)
    def _(step):
        remote(meta_vmem, meta_all.at[row], meta_send.at[step], meta_recv.at[row], peer(step)).wait_send()

    for h in range(2):
        @pl.when(core == 0)
        def _():
            row_copy(h, 2, sibling).wait_send()

        @pl.when(col == 0)
        def _():
            row_copy(h, 0, up).wait_send()
            row_copy(h, 1, down).wait_send()

        @pl.when(mine & (owner_dz == 0))
        def _():
            for kind in range(4):
                source_copy(h, kind).wait_send()

        @pl.when(mine & (owner_dz != 0))
        def _():
            col_copy(x % 2, h, 2).wait_send()
            col_copy(x % 2, h, 3).wait_send()

    @pl.when(col == 2)
    def _():
        row_copy(0, 0, up).wait_send()

    @pl.when(col == 6)
    def _():
        row_copy(1, 1, down).wait_send()

    @pl.when(mine & (owner_dz == 1))
    def _():
        col_copy(x % 2, 0, 0).wait_send()

    @pl.when(mine & (owner_dz == 3))
    def _():
        col_copy(x % 2, 1, 1).wait_send()

    for j in range(2):
        dx = (x + 4 - (2 * core + j)) % 4

        @pl.when(dx == 1)
        def _():
            col_copy(j, 0, 2).wait_send()

        @pl.when(dx == 3)
        def _():
            col_copy(j, 1, 3).wait_send()


def exchange(meta, child_front, child_inverse, front, panel_inverse):
    vmem = pl.BlockSpec(memory_space=pltpu.VMEM)
    dma = pltpu.SemaphoreType.DMA
    return pl.pallas_call(
        exchange_kernel,
        out_shape=(
            pltpu.VMEM((RUNS, 2, 2, TILE, TILE), BF16),
            pltpu.VMEM((RUNS, 2, 2, TILE, TILE), BF16),
            pltpu.VMEM((ROWS, PANEL), BF16),
            pltpu.VMEM(front.shape, F32),
            pltpu.VMEM((RUNS, 8, 128), jnp.int32),
        ),
        in_specs=[
            pl.BlockSpec(memory_space=pltpu.SMEM), vmem, pl.BlockSpec(memory_space=pl.ANY),
            pl.BlockSpec(memory_space=pl.ANY), pl.BlockSpec(memory_space=pl.ANY), vmem,
        ],
        out_specs=(vmem, vmem, vmem, vmem, vmem),
        scratch_shapes=[
            pltpu.VMEM((SLOTS, TILE, PIV), BF16),
            pltpu.VMEM((SLOTS, TILE, PIV), BF16),
            pltpu.VMEM((4 * TILE, PIV), BF16),
            pltpu.VMEM((2, RUNS, 2, 2, TILE, TILE), BF16),
            pltpu.VMEM((ROWS, PANEL), F32),
            pltpu.VMEM((2, ROWS, PANEL), BF16),
            pltpu.VMEM((PIV, PIV), BF16),
            pltpu.SMEM((RUNS, 8, 128), jnp.int32),
            dma((2, 4)), dma((2, 2)), dma((4, 4)), dma((SLOTS,)),
            dma((2, RUNS)), dma((2, RUNS)), dma((RUNS,)), dma((RUNS,)), dma((4,)),
            dma((3, 2)), dma((2,)), dma((4, 2, 2)), dma((2, 2)),
        ],
        compiler_params=pltpu.CompilerParams(
            collective_id=0, has_side_effects=True, vmem_limit_bytes=48 << 20
        ),
        name="exchange",
    )(meta, meta, child_front.reshape(1, PART // TILE, TILE, PIV), child_inverse, front, panel_inverse)


def finish_kernel(
    meta_ref, work, arrived_first, arrived_second, panel_row, trailing, panel_out, result, out_sem
):
    row = lax.axis_index("row")
    col = lax.axis_index("col")
    stores = []
    for half, arrived in enumerate((arrived_first, arrived_second)):
        span = pl.ds(half * ROWS, ROWS)
        result[:, span] = work[:, span]

        @pl.loop(0, RUNS)
        def _(child):
            for a in range(2):
                tile_row = meta_ref[child, 1, 2 * row + a]
                for b in range(2):
                    tile_col = meta_ref[child, 1, 4 * col + 2 * half + b]

                    @pl.when((tile_row >= 0) & (tile_col >= 0))
                    def _():
                        place = (tile_rows(tile_row), tile_rows(half * RUN + tile_col))
                        result[place] += arrived[child, a, b].astype(F32)

        store = pltpu.make_async_copy(result.at[:, span], trailing.at[:, span], out_sem.at[half])
        store.start()
        stores.append(store)
    panel_out[...] = panel_row[...].astype(F32)
    for store in stores:
        store.wait()


def finish(meta_all, work, arrived_first, arrived_second, panel_row):
    vmem = pl.BlockSpec(memory_space=pltpu.VMEM)
    return pl.pallas_call(
        finish_kernel,
        out_shape=(
            jax.ShapeDtypeStruct(work.shape, F32), jax.ShapeDtypeStruct((ROWS, PANEL), F32)
        ),
        in_specs=[pl.BlockSpec(memory_space=pltpu.SMEM), vmem, vmem, vmem, vmem],
        out_specs=(pl.BlockSpec(memory_space=pl.ANY), vmem),
        scratch_shapes=[
            pltpu.VMEM(work.shape, F32), pltpu.SemaphoreType.DMA((2,)),
        ],
        compiler_params=pltpu.CompilerParams(vmem_limit_bytes=16 << 20),
        name="finish",
    )(meta_all, work, arrived_first, arrived_second, panel_row)


def slot_table(child_index, child_size):
    places = jnp.arange(SLOTS, dtype=jnp.int32)
    tiles = jnp.where(places < child_size[0], child_index[0], RUN * RUNS)
    before = jnp.sum((tiles[None, :] < RUN * (places // 2)[:, None]).astype(jnp.int32), axis=1)
    place = jnp.minimum(before + places % 2, SLOTS - 1)
    picked = jnp.sum(jnp.where(place[:, None] == places[None, :], tiles[None, :], 0), axis=1)
    local = picked - RUN * (places // 2)
    live = (local >= 0) & (local < RUN) & (before + places % 2 < SLOTS)
    wanted = jnp.arange(RUN * RUNS, dtype=jnp.int32)
    match = (picked[None, :] == wanted[:, None]) & live[None, :]
    slot = jnp.sum(jnp.where(match, places % 2, 0), axis=1)
    held = jnp.sum(match.astype(jnp.int32), axis=1)

    def lane(values):
        return jnp.pad(values, (0, 128 - values.shape[0]))

    table = jnp.stack([lane(place), lane(jnp.where(live, local, -1)), lane(slot), lane(held)])
    return jnp.pad(table, ((0, 4), (0, 0)))


def shards(child_front, child_inverse, child_index, child_size, front, panel_inverse):
    meta = slot_table(child_index, child_size)
    arrived_first, arrived_second, panel_row, work, meta_all = exchange(
        meta, child_front, child_inverse, front, panel_inverse
    )
    return finish(meta_all, work, arrived_first, arrived_second, panel_row)


def solution(mesh):
    in_specs = (
        P("row", "col", None),
        P("row", None, None),
        P("row", None),
        P("row"),
        P("row", "col"),
        P(),
    )
    out_specs = (P("row", "col"), P("row", None))
    return jax.shard_map(shards, mesh=mesh, in_specs=in_specs, out_specs=out_specs, check_vma=False)
```

time: 141 us -> 129 us (0.915)
  the two profiles are of different devices: /device:TPU:110 before, /device:TPU:20 now
where the time goes in v2:
time: 129 us
  Pallas kernels  126 us (98%)
  between operations  1.49 us (1%)
    pallas_call x1, Pallas kernels, exchange(): pl.pallas_call(exchange_kernel, out_shape=(pltpu.VMEM((RUNS, 2, 2, TILE,...  120 us
    pallas_call x1, Pallas kernels, finish(): pl.pallas_call(finish_kernel, out_shape=(jax.ShapeDtypeStruct(work.shape,...  5.98 us

profile of v2, /device:TPU:20, one launch (start us, length us, event | category | flops | bytes accessed | tf_op | source)
XLA Modules:
  0.0 128.9 jit_solution(9253101774427676910)
XLA Ops:
  1.3 0.7 fusion.2
  1.9 0.2 convert_reduce_fusion.1
  2.1 0.2 select_reduce_fusion.1
  2.4 0.1 select_reduce_fusion
  2.5 0.6 pad.22.meta_ref.meta_vmem
  3.1 119.6 %exchange.1 = (bf16[16,2,2,128,128]{4,3,2,1,0:T(8,128)(2,1)S(1)}, bf16[16,2,2,128,128]{4,3,2,1,0:T(8,128)(2,1)S(1)}, bf16[640,256]{1,0:T(8,128)(2,1)S(1)}, f32[640,1280]{1,0:T(8,128)S(1)}, s32[16,8,128]{2,1,0:T(8,128)S(1)}) custom-call(s32[8,128]{1,0:T(8,128)} %pad.22.meta_ref.meta_vmem, s32[8,128]{1,0:T(8,128)} %pad.22.meta_ref.meta_vmem, ...), custom_call_target="tpu_custom_call" | custom-call | tf_op jit(solution)/shard_map/exchange/pallas_call | solution.py:411
  122.7 6.0 %finish.1 = (f32[640,1280]{1,0:T(8,128)}, f32[640,256]{1,0:T(8,128)}) custom-call(s32[16,8,128]{2,1,0:T(8,128)S(1)} %get-tuple-element.7.meta_ref, f32[640,1280]{1,0:T(8,128)S(1)} %get-tuple-element.8.work, bf16[16,2,2,128,128]{4,3,2,1,0:T(8,128)(2,1)S(1)} %get-tuple-element.9.arrived_first, ...), custom_call_target="tpu_custom_call" | custom-call | tf_op jit(solution)/shard_map/finish/pallas_call | solution.py:477
  (7 shorter events, 0.0 us)

commit v3 on v2

--- a/solution.py
+++ b/solution.py
@@ -20,7 +20,6 @@
 HALF = ROWS // 2
 NT = (((1,), (1,)), ((), ()))
 NEAR = (1, 3, 4, 12, 5, 15, 7, 13, 2, 8, 9, 6, 11, 14, 10)
-EARLY, MIDDLE = 4, 9
 BF16 = jnp.bfloat16
 F32 = jnp.float32
 
@@ -45,6 +44,7 @@
     up = {"row": row, "col": ((y + 1) % 4) * 2 + core}
     down = {"row": row, "col": ((y + 3) % 4) * 2 + core}
     sibling = {"row": row, "col": y * 2 + 1 - core}
+    opposite = {"row": row, "col": ((y + 2) % 4) * 2 + core}
 
     def peer_row(step):
         return ((z + step // 4) % 4) * 4 + (x + step % 4) % 4
@@ -59,7 +59,7 @@
         )
 
     barrier = pltpu.get_barrier_semaphore()
-    for device in (up, down, sibling):
+    for device in (up, down, sibling, opposite):
         pl.semaphore_signal(barrier, inc=1, device_id=device, device_id_type=pl.DeviceIdType.MESH)
 
     @pl.loop(1, RUNS)
@@ -72,7 +72,7 @@
     child_in.start()
     front_in = pltpu.make_async_copy(front_ref, work, local_sem.at[0])
     front_in.start()
-    pl.semaphore_wait(barrier, 3 + RUNS - 1)
+    pl.semaphore_wait(barrier, 4 + RUNS - 1)
 
     def part_copy(c, t, send, device):
         tile = children.at[c * 4 + t]
@@ -194,34 +194,31 @@
                 @pl.when(eager)
                 def _():
                     block_copy(half, held).start()
-            held = step if half == 0 or step in NEAR[:EARLY] else None
-        if held is not None:
-            @pl.when(eager)
-            def _():
-                block_copy(half, held).start()
+            held = step
+        @pl.when(eager)
+        def _():
+            block_copy(half, held).start()
 
     @pl.when(col == 1)
     def _():
         for half in range(2):
-            for step in NEAR if half == 0 else NEAR[:EARLY]:
+            for step in NEAR:
                 block_copy(half, step).start()
 
-    def send_late(first, last):
-        for step in NEAR[first:last]:
-            block_copy(1, step).start()
+    def wait_block(half, step):
+        source = peer_row(step)
+        remote(
+            outgoing.at[half, step], arrived[half].at[source],
+            block_send.at[half, step], block_recv.at[half, source], peer(step),
+        ).wait_recv()
 
     def wait_blocks(half):
         @pl.loop(1, RUNS)
         def _(step):
-            source = peer_row(step)
-            remote(
-                outgoing.at[half, step], arrived[half].at[source],
-                block_send.at[half, step], block_recv.at[half, source], peer(step),
-            ).wait_recv()
+            wait_block(half, step)
 
     meta_in.wait()
     front_in.wait()
-    wait_blocks(0)
 
     def half_rows(h):
         return pl.ds(h * HALF, HALF)
@@ -234,22 +231,24 @@
 
     def recv_row(h):
         row_copy(h, 0, sibling).wait_recv()
+
+    wait_blocks(0)
 
     @pl.when(col == 0)
     def _():
         for j in range(PANEL // TILE):
             @pl.loop(0, RUN)
             def _(i):
-                def add(child, total):
+                place = (tile_rows(i), pl.ds(j * TILE, TILE))
+                total = work[place]
+                for child in range(RUNS):
                     tile = arrived_first[
                         child, meta_smem[child, 2, RUN * row + i], meta_smem[child, 2, j]
                     ]
                     here = meta_smem[child, 3, RUN * row + i] * meta_smem[child, 3, j]
                     keep = jnp.full((TILE, TILE), here, jnp.int32) != 0
-                    return total + jnp.where(keep, tile.astype(F32), 0.0)
-
-                start = work[tile_rows(i), pl.ds(j * TILE, TILE)]
-                panel[tile_rows(i), pl.ds(j * TILE, TILE)] = lax.fori_loop(0, RUNS, add, start, unroll=4)
+                    total += jnp.where(keep, tile.astype(F32), 0.0)
+                panel[place] = total
 
         for h in range(2):
             panel_row[half_rows(h), :] = lax.dot_general(
@@ -257,7 +256,7 @@
                 preferred_element_type=F32,
             ).astype(BF16)
 
-    kinds = (peer(4), peer(12), peer(1), peer(3))
+    kinds = (peer(4), peer(12), peer(8), peer(1), peer(3), peer(2))
     owner_dz = (z + 4 - y) % 4
     mine = (x // 2) == core
 
@@ -279,27 +278,19 @@
         def _():
             row_copy(h, 0, up).start()
             row_copy(h, 1, down).start()
+            row_copy(h, 2, opposite).start()
 
         @pl.when((core == 1) | (y > 0))
         def _():
             recv_row(h)
 
-        if h == 0:
-            @pl.when(col == 2)
-            def _():
-                row_copy(h, 0, up).start()
-        else:
-            @pl.when(col == 6)
-            def _():
-                row_copy(h, 1, down).start()
-
         @pl.when(core == 0)
         def _():
-            row_copy(h, 2, sibling).start()
+            row_copy(h, 3, sibling).start()
 
         @pl.when(mine & (owner_dz == 0))
         def _():
-            for kind in range(4):
+            for kind in range(6):
                 source_copy(h, kind).start()
             panel_col[x % 2, half_rows(h), :] = panel_row[half_rows(h), :]
 
@@ -307,35 +298,19 @@
         @pl.when(mine & (owner_dz != 0))
         def _():
             recv_col(x % 2, h)
-            if h == 0:
-                @pl.when(owner_dz == 1)
-                def _():
-                    col_copy(x % 2, h, 0).start()
-            else:
-                @pl.when(owner_dz == 3)
-                def _():
-                    col_copy(x % 2, h, 1).start()
-            col_copy(x % 2, h, 2).start()
-            col_copy(x % 2, h, 3).start()
+            for kind in range(3, 6):
+                col_copy(x % 2, h, kind).start()
 
     def x_stage(h):
         for j in range(2):
-            dx = (x + 4 - (2 * core + j)) % 4
-
-            @pl.when(dx != 0)
+            @pl.when((x + 4 - (2 * core + j)) % 4 != 0)
             def _():
                 recv_col(j, h)
 
-            @pl.when(dx == (1 if h == 0 else 3))
-            def _():
-                col_copy(j, h, 2 if h == 0 else 3).start()
-
     row_stage(0)
     row_stage(1)
-    send_late(EARLY, MIDDLE)
     z_stage(0)
     z_stage(1)
-    send_late(MIDDLE, RUNS - 1)
     x_stage(0)
     x_stage(1)
 
@@ -360,49 +335,23 @@
     for h in range(2):
         @pl.when(core == 0)
         def _():
-            row_copy(h, 2, sibling).wait_send()
+            row_copy(h, 3, sibling).wait_send()
 
         @pl.when(col == 0)
         def _():
             row_copy(h, 0, up).wait_send()
             row_copy(h, 1, down).wait_send()
+            row_copy(h, 2, opposite).wait_send()
 
         @pl.when(mine & (owner_dz == 0))
         def _():
-            for kind in range(4):
+            for kind in range(6):
                 source_copy(h, kind).wait_send()
 
         @pl.when(mine & (owner_dz != 0))
         def _():
-            col_copy(x % 2, h, 2).wait_send()
-            col_copy(x % 2, h, 3).wait_send()
-
-    @pl.when(col == 2)
-    def _():
-        row_copy(0, 0, up).wait_send()
-
-    @pl.when(col == 6)
-    def _():
-        row_copy(1, 1, down).wait_send()
-
-    @pl.when(mine & (owner_dz == 1))
-    def _():
-        col_copy(x % 2, 0, 0).wait_send()
-
-    @pl.when(mine & (owner_dz == 3))
-    def _():
-        col_copy(x % 2, 1, 1).wait_send()
-
-    for j in range(2):
-        dx = (x + 4 - (2 * core + j)) % 4
-
-        @pl.when(dx == 1)
-        def _():
-            col_copy(j, 0, 2).wait_send()
-
-        @pl.when(dx == 3)
-        def _():
-            col_copy(j, 1, 3).wait_send()
+            for kind in range(3, 6):
+                col_copy(x % 2, h, kind).wait_send()
 
 
 def exchange(meta, child_front, child_inverse, front, panel_inverse):
@@ -433,7 +382,7 @@
             pltpu.SMEM((RUNS, 8, 128), jnp.int32),
             dma((2, 4)), dma((2, 2)), dma((4, 4)), dma((SLOTS,)),
             dma((2, RUNS)), dma((2, RUNS)), dma((RUNS,)), dma((RUNS,)), dma((4,)),
-            dma((3, 2)), dma((2,)), dma((4, 2, 2)), dma((2, 2)),
+            dma((4, 2)), dma((2,)), dma((6, 2, 2)), dma((2, 2)),
         ],
         compiler_params=pltpu.CompilerParams(
             collective_id=0, has_side_effects=True, vmem_limit_bytes=48 << 20

time: 129 us -> 124 us (0.961)
  Pallas kernels: 126 us -> 120 us
    pallas_call x1, Pallas kernels: 120 us -> 114 us  [exchange(): pl.pallas_call(exchange_kernel, out_shape=(pltpu.VMEM((RUNS, 2, 2, TILE,...]
where the time goes in v3:
time: 124 us
  Pallas kernels  120 us (97%)
  between operations  1.49 us (1%)
    pallas_call x1, Pallas kernels, exchange(): pl.pallas_call(exchange_kernel, out_shape=(pltpu.VMEM((RUNS, 2, 2, TILE,...  114 us
    pallas_call x1, Pallas kernels, finish(): pl.pallas_call(finish_kernel, out_shape=(jax.ShapeDtypeStruct(work.shape,...  5.99 us

profile of v3, /device:TPU:20, one launch (start us, length us, event | category | flops | bytes accessed | tf_op | source)
XLA Modules:
  0.0 123.6 jit_solution(11729219237601168739)
XLA Ops:
  1.3 0.7 fusion.2
  1.9 0.2 convert_reduce_fusion.1
  2.1 0.2 select_reduce_fusion.1
  2.4 0.1 select_reduce_fusion
  2.5 0.6 pad.22.meta_ref.meta_vmem
  3.1 114.4 %exchange.1 = (bf16[16,2,2,128,128]{4,3,2,1,0:T(8,128)(2,1)S(1)}, bf16[16,2,2,128,128]{4,3,2,1,0:T(8,128)(2,1)S(1)}, bf16[640,256]{1,0:T(8,128)(2,1)S(1)}, f32[640,1280]{1,0:T(8,128)S(1)}, s32[16,8,128]{2,1,0:T(8,128)S(1)}) custom-call(s32[8,128]{1,0:T(8,128)} %pad.22.meta_ref.meta_vmem, s32[8,128]{1,0:T(8,128)} %pad.22.meta_ref.meta_vmem, ...), custom_call_target="tpu_custom_call" | custom-call | tf_op jit(solution)/shard_map/exchange/pallas_call | solution.py:360
  117.4 6.0 %finish.1 = (f32[640,1280]{1,0:T(8,128)}, f32[640,256]{1,0:T(8,128)}) custom-call(s32[16,8,128]{2,1,0:T(8,128)S(1)} %get-tuple-element.7.meta_ref, f32[640,1280]{1,0:T(8,128)S(1)} %get-tuple-element.8.work, bf16[16,2,2,128,128]{4,3,2,1,0:T(8,128)(2,1)S(1)} %get-tuple-element.9.arrived_first, ...), custom_call_target="tpu_custom_call" | custom-call | tf_op jit(solution)/shard_map/finish/pallas_call | solution.py:426
  (7 shorter events, 0.0 us)

commit v4 on v3

--- a/solution.py
+++ b/solution.py
@@ -28,10 +28,36 @@
     return pl.ds(pl.multiple_of(index * TILE, TILE), TILE)
 
 
+def slot_table(size_ref, index_ref, index_row, table):
+    index_row[...] = jnp.zeros_like(index_row)
+    index_row[0:1, 0:SLOTS] = index_ref[...]
+    lane = lax.broadcasted_iota(jnp.int32, (1, 128), 1)
+    tiles = jnp.where(lane < size_ref[0], index_row[0:1, :], RUN * RUNS)
+    tiles = jnp.transpose(jnp.broadcast_to(tiles, (128, 128)))[:SLOTS]
+    places = lax.broadcasted_iota(jnp.int32, (SLOTS, 128), 0)
+
+    def total(kept, values):
+        return jnp.sum(jnp.where(kept, values, 0), axis=0, keepdims=True)
+
+    one = jnp.ones_like(tiles)
+    first = RUN * (lane >> 1)
+    order = total(tiles < first, one) + (lane & 1)
+    place = jnp.minimum(order, SLOTS - 1)
+    local = total(places == place, tiles) - first
+    live = (local >= 0) & (local < RUN) & (order < SLOTS)
+    same = tiles == lane
+    run_first = RUN * ((lane * 205) >> 10)
+    held = total(same, one)
+    slot = total(same, places) - total(tiles < run_first, one)
+    slot = jnp.minimum(jnp.maximum(jnp.where(held > 0, slot, 0), 0), 1)
+    for i, values in enumerate((place, jnp.where(live, local, -1), slot, held)):
+        table[i:i + 1, :] = values
+
+
 def exchange_kernel(
-    meta_ref, meta_vmem, child_ref, inverse_hbm, front_ref, panel_inverse_ref,
+    size_ref, index_ref, child_ref, inverse_hbm, front_ref, panel_inverse_ref,
     arrived_first, arrived_second, panel_row, work, meta_all,
-    children, factor, column_tiles, outgoing, panel, panel_col, inverse_ref, meta_smem,
+    children, factor, column_tiles, outgoing, panel, panel_col, inverse_ref, meta_smem, index_row, meta_vmem,
     own_send, pass_send, sibling_send, gather_recv,
     block_send, block_recv, meta_send, meta_recv, local_sem,
     row_send, row_recv, col_send, col_recv,
@@ -72,6 +98,7 @@
     child_in.start()
     front_in = pltpu.make_async_copy(front_ref, work, local_sem.at[0])
     front_in.start()
+    slot_table(size_ref, index_ref, index_row, meta_vmem)
     pl.semaphore_wait(barrier, 4 + RUNS - 1)
 
     def part_copy(c, t, send, device):
@@ -140,6 +167,18 @@
         recv_part(twins[0], a)
         recv_part(twins[1], b)
         make_factor((twins[0], a), (twins[1], b))
+    meta_own.wait()
+
+    @pl.loop(1, RUNS)
+    def _(step):
+        source = peer_row(step)
+        remote(
+            meta_vmem, meta_all.at[source], meta_send.at[step], meta_recv.at[source], peer(step)
+        ).wait_recv()
+
+    meta_in = pltpu.make_async_copy(meta_all, meta_smem, local_sem.at[1])
+    meta_in.start()
+
     for a, b in ((0, 2), (1, 3)):
         for t in (a, b):
             recv_part(across, t)
@@ -149,24 +188,14 @@
             recv_part(twins[2], t)
         make_factor((twins[2], a), (twins[2], b))
 
-    meta_own.wait()
-
-    @pl.loop(1, RUNS)
-    def _(step):
-        source = peer_row(step)
-        remote(
-            meta_vmem, meta_all.at[source], meta_send.at[step], meta_recv.at[source], peer(step)
-        ).wait_recv()
-
-    meta_in = pltpu.make_async_copy(meta_all, meta_smem, local_sem.at[1])
-    meta_in.start()
+    meta_in.wait()
 
     for slot in range(4):
-        column_tiles[pl.ds(slot * TILE, TILE), :] = factor[meta_ref[0, col * 4 + slot]]
+        column_tiles[pl.ds(slot * TILE, TILE), :] = factor[meta_smem[row, 0, col * 4 + slot]]
 
     def block(half, target):
-        first = factor[meta_ref[0, 2 * target]]
-        second = factor[meta_ref[0, 2 * target + 1]]
+        first = factor[meta_smem[row, 0, 2 * target]]
+        second = factor[meta_smem[row, 0, 2 * target + 1]]
         rows = jnp.concatenate([first, second], axis=0)
         product = lax.dot_general(
             rows, column_tiles[pl.ds(half * PAIR, PAIR), :], NT, preferred_element_type=F32
@@ -217,7 +246,6 @@
         def _(step):
             wait_block(half, step)
 
-    meta_in.wait()
     front_in.wait()
 
     def half_rows(h):
@@ -354,7 +382,7 @@
                 col_copy(x % 2, h, kind).wait_send()
 
 
-def exchange(meta, child_front, child_inverse, front, panel_inverse):
+def exchange(child_size, child_index, child_front, child_inverse, front, panel_inverse):
     vmem = pl.BlockSpec(memory_space=pltpu.VMEM)
     dma = pltpu.SemaphoreType.DMA
     return pl.pallas_call(
@@ -364,7 +392,7 @@
             pltpu.VMEM((RUNS, 2, 2, TILE, TILE), BF16),
             pltpu.VMEM((ROWS, PANEL), BF16),
             pltpu.VMEM(front.shape, F32),
-            pltpu.VMEM((RUNS, 8, 128), jnp.int32),
+            pltpu.VMEM((RUNS, 4, 128), jnp.int32),
         ),
         in_specs=[
             pl.BlockSpec(memory_space=pltpu.SMEM), vmem, pl.BlockSpec(memory_space=pl.ANY),
@@ -379,7 +407,9 @@
             pltpu.VMEM((ROWS, PANEL), F32),
             pltpu.VMEM((2, ROWS, PANEL), BF16),
             pltpu.VMEM((PIV, PIV), BF16),
-            pltpu.SMEM((RUNS, 8, 128), jnp.int32),
+            pltpu.SMEM((RUNS, 4, 128), jnp.int32),
+            pltpu.VMEM((8, 128), jnp.int32),
+            pltpu.VMEM((4, 128), jnp.int32),
             dma((2, 4)), dma((2, 2)), dma((4, 4)), dma((SLOTS,)),
             dma((2, RUNS)), dma((2, RUNS)), dma((RUNS,)), dma((RUNS,)), dma((4,)),
             dma((4, 2)), dma((2,)), dma((6, 2, 2)), dma((2, 2)),
@@ -388,7 +418,7 @@
             collective_id=0, has_side_effects=True, vmem_limit_bytes=48 << 20
         ),
         name="exchange",
-    )(meta, meta, child_front.reshape(1, PART // TILE, TILE, PIV), child_inverse, front, panel_inverse)
+    )(child_size, child_index, child_front.reshape(1, PART // TILE, TILE, PIV), child_inverse, front, panel_inverse)
 
 
 def finish_kernel(
@@ -438,30 +468,9 @@
     )(meta_all, work, arrived_first, arrived_second, panel_row)
 
 
-def slot_table(child_index, child_size):
-    places = jnp.arange(SLOTS, dtype=jnp.int32)
-    tiles = jnp.where(places < child_size[0], child_index[0], RUN * RUNS)
-    before = jnp.sum((tiles[None, :] < RUN * (places // 2)[:, None]).astype(jnp.int32), axis=1)
-    place = jnp.minimum(before + places % 2, SLOTS - 1)
-    picked = jnp.sum(jnp.where(place[:, None] == places[None, :], tiles[None, :], 0), axis=1)
-    local = picked - RUN * (places // 2)
-    live = (local >= 0) & (local < RUN) & (before + places % 2 < SLOTS)
-    wanted = jnp.arange(RUN * RUNS, dtype=jnp.int32)
-    match = (picked[None, :] == wanted[:, None]) & live[None, :]
-    slot = jnp.sum(jnp.where(match, places % 2, 0), axis=1)
-    held = jnp.sum(match.astype(jnp.int32), axis=1)
-
-    def lane(values):
-        return jnp.pad(values, (0, 128 - values.shape[0]))
-
-    table = jnp.stack([lane(place), lane(jnp.where(live, local, -1)), lane(slot), lane(held)])
-    return jnp.pad(table, ((0, 4), (0, 0)))
-
-
 def shards(child_front, child_inverse, child_index, child_size, front, panel_inverse):
-    meta = slot_table(child_index, child_size)
     arrived_first, arrived_second, panel_row, work, meta_all = exchange(
-        meta, child_front, child_inverse, front, panel_inverse
+        child_size, child_index, child_front, child_inverse, front, panel_inverse
     )
     return finish(meta_all, work, arrived_first, arrived_second, panel_row)
 

time: 124 us -> 120 us (0.968)
  Pallas kernels: 120 us -> 118 us
    pallas_call x1, Pallas kernels: 114 us -> 113 us  [exchange(): pl.pallas_call(exchange_kernel, out_shape=(pltpu.VMEM((RUNS, 2, 2, TILE,...]
where the time goes in v4:
time: 120 us
  Pallas kernels  118 us (98%)
  between operations  1.45 us (1%)
    pallas_call x1, Pallas kernels, exchange(): pl.pallas_call(exchange_kernel, out_shape=(pltpu.VMEM((RUNS, 2, 2, TILE,...  113 us
    pallas_call x1, Pallas kernels, finish(): pl.pallas_call(finish_kernel, out_shape=(jax.ShapeDtypeStruct(work.shape,...  5.41 us

profile of v4, /device:TPU:20, one launch (start us, length us, event | category | flops | bytes accessed | tf_op | source)
XLA Modules:
  0.0 119.8 jit_solution(7349593615368703861)
XLA Ops:
  1.3 113.0 %exchange.1 = (bf16[16,2,2,128,128]{4,3,2,1,0:T(8,128)(2,1)S(1)}, bf16[16,2,2,128,128]{4,3,2,1,0:T(8,128)(2,1)S(1)}, bf16[640,256]{1,0:T(8,128)(2,1)S(1)}, f32[640,1280]{1,0:T(8,128)S(1)}, s32[16,4,128]{2,1,0:T(4,128)S(1)}) custom-call(s32[1]{0:T(128)S(6)} %copy.8.size_ref, s32[1,32]{1,0:T(1,128)} %index_ref.1, bf16[1,4,128,1024]{3,2,1,0:T(8,128)(2,1)} %bitcast.1, ...), custom_call_target="tpu_custom_call" | custom-call | tf_op jit(solution)/shard_map/exchange/pallas_call | solution.py:388
  114.3 5.4 %finish.1 = (f32[640,1280]{1,0:T(8,128)}, f32[640,256]{1,0:T(8,128)}) custom-call(s32[16,4,128]{2,1,0:T(4,128)S(1)} %get-tuple-element.7.meta_ref, f32[640,1280]{1,0:T(8,128)S(1)} %get-tuple-element.8.work, bf16[16,2,2,128,128]{4,3,2,1,0:T(8,128)(2,1)S(1)} %get-tuple-element.9.arrived_first, ...), custom_call_target="tpu_custom_call" | custom-call | tf_op jit(solution)/shard_map/finish/pallas_call | solution.py:456

commit v5 on v4

--- a/solution.py
+++ b/solution.py
@@ -17,7 +17,7 @@
 PART = 512
 ROWS = RUN * TILE
 PAIR = 2 * TILE
-HALF = ROWS // 2
+HALF = ROWS // 4
 NT = (((1,), (1,)), ((), ()))
 NEAR = (1, 3, 4, 12, 5, 15, 7, 13, 2, 8, 9, 6, 11, 14, 10)
 BF16 = jnp.bfloat16
@@ -278,7 +278,7 @@
                     total += jnp.where(keep, tile.astype(F32), 0.0)
                 panel[place] = total
 
-        for h in range(2):
+        for h in range(4):
             panel_row[half_rows(h), :] = lax.dot_general(
                 panel[half_rows(h), :], panel_inverse_ref[...], NT, precision=lax.Precision.HIGHEST,
                 preferred_element_type=F32,
@@ -329,24 +329,21 @@
             for kind in range(3, 6):
                 col_copy(x % 2, h, kind).start()
 
-    def x_stage(h):
-        for j in range(2):
-            @pl.when((x + 4 - (2 * core + j)) % 4 != 0)
-            def _():
+    for h in range(4):
+        row_stage(h)
+    for h in range(4):
+        z_stage(h)
+    for j in (x % 2, 1 - x % 2):
+        @pl.when(x != 2 * core + j)
+        def _():
+            for h in range(4):
                 recv_col(j, h)
 
-    row_stage(0)
-    row_stage(1)
-    z_stage(0)
-    z_stage(1)
-    x_stage(0)
-    x_stage(1)
-
-    for half in range(2):
-        span = pl.ds(half * ROWS, ROWS)
+        span = pl.ds(pl.multiple_of(j * ROWS, TILE), ROWS)
         work[:, span] -= lax.dot_general(
-            panel_row[...], panel_col[half], NT, preferred_element_type=F32
-        )
+            panel_row[...], panel_col[j], NT, preferred_element_type=F32
+        )
+
     wait_blocks(1)
 
     for copy in sent:
@@ -360,7 +357,7 @@
     def _(step):
         remote(meta_vmem, meta_all.at[row], meta_send.at[step], meta_recv.at[row], peer(step)).wait_send()
 
-    for h in range(2):
+    for h in range(4):
         @pl.when(core == 0)
         def _():
             row_copy(h, 3, sibling).wait_send()
@@ -412,7 +409,7 @@
             pltpu.VMEM((4, 128), jnp.int32),
             dma((2, 4)), dma((2, 2)), dma((4, 4)), dma((SLOTS,)),
             dma((2, RUNS)), dma((2, RUNS)), dma((RUNS,)), dma((RUNS,)), dma((4,)),
-            dma((4, 2)), dma((2,)), dma((6, 2, 2)), dma((2, 2)),
+            dma((4, 4)), dma((4,)), dma((6, 4, 2)), dma((2, 4)),
         ],
         compiler_params=pltpu.CompilerParams(
             collective_id=0, has_side_effects=True, vmem_limit_bytes=48 << 20
@@ -437,11 +434,13 @@
                 tile_row = meta_ref[child, 1, 2 * row + a]
                 for b in range(2):
                     tile_col = meta_ref[child, 1, 4 * col + 2 * half + b]
-
-                    @pl.when((tile_row >= 0) & (tile_col >= 0))
-                    def _():
-                        place = (tile_rows(tile_row), tile_rows(half * RUN + tile_col))
-                        result[place] += arrived[child, a, b].astype(F32)
+                    live = (tile_row >= 0) & (tile_col >= 0)
+                    keep = jnp.full((TILE, TILE), live.astype(jnp.int32), jnp.int32) != 0
+                    place = (
+                        tile_rows(jnp.maximum(tile_row, 0)),
+                        tile_rows(half * RUN + jnp.maximum(tile_col, 0)),
+                    )
+                    result[place] += jnp.where(keep, arrived[child, a, b].astype(F32), 0.0)
 
         store = pltpu.make_async_copy(result.at[:, span], trailing.at[:, span], out_sem.at[half])
         store.start()

time: 120 us -> 119 us (level)
  no operation moved by 1% of the time
where the time goes in v5:
time: 119 us
  Pallas kernels  117 us (98%)
  between operations  1.45 us (1%)
    pallas_call x1, Pallas kernels, exchange(): pl.pallas_call(exchange_kernel, out_shape=(pltpu.VMEM((RUNS, 2, 2, TILE,...  113 us
    pallas_call x1, Pallas kernels, finish(): pl.pallas_call(finish_kernel, out_shape=(jax.ShapeDtypeStruct(work.shape,...  4.72 us

profile of v5, /device:TPU:20, one launch (start us, length us, event | category | flops | bytes accessed | tf_op | source)
XLA Modules:
  0.0 118.8 jit_solution(15924780675330100606)
XLA Ops:
  1.3 112.7 %exchange.1 = (bf16[16,2,2,128,128]{4,3,2,1,0:T(8,128)(2,1)S(1)}, bf16[16,2,2,128,128]{4,3,2,1,0:T(8,128)(2,1)S(1)}, bf16[640,256]{1,0:T(8,128)(2,1)S(1)}, f32[640,1280]{1,0:T(8,128)S(1)}, s32[16,4,128]{2,1,0:T(4,128)S(1)}) custom-call(s32[1]{0:T(128)S(6)} %copy.8.size_ref, s32[1,32]{1,0:T(1,128)} %index_ref.1, bf16[1,4,128,1024]{3,2,1,0:T(8,128)(2,1)} %bitcast.1, ...), custom_call_target="tpu_custom_call" | custom-call | tf_op jit(solution)/shard_map/exchange/pallas_call | solution.py:385
  114.0 4.7 %finish.1 = (f32[640,1280]{1,0:T(8,128)}, f32[640,256]{1,0:T(8,128)}) custom-call(s32[16,4,128]{2,1,0:T(4,128)S(1)} %get-tuple-element.7.meta_ref, f32[640,1280]{1,0:T(8,128)S(1)} %get-tuple-element.8.work, bf16[16,2,2,128,128]{4,3,2,1,0:T(8,128)(2,1)S(1)} %get-tuple-element.9.arrived_first, ...), custom_call_target="tpu_custom_call" | custom-call | tf_op jit(solution)/shard_map/finish/pallas_call | solution.py:455

commit v6 on v5

--- a/solution.py
+++ b/solution.py
@@ -318,7 +318,7 @@
 
         @pl.when(mine & (owner_dz == 0))
         def _():
-            for kind in range(6):
+            for kind in (2, 0, 1, 5, 3, 4):
                 source_copy(h, kind).start()
             panel_col[x % 2, half_rows(h), :] = panel_row[half_rows(h), :]
 
@@ -326,7 +326,7 @@
         @pl.when(mine & (owner_dz != 0))
         def _():
             recv_col(x % 2, h)
-            for kind in range(3, 6):
+            for kind in (5, 3, 4):
                 col_copy(x % 2, h, kind).start()
 
     for h in range(4):

time: 119 us -> 118 us (level)
    pallas_call x1, Pallas kernels: 113 us -> 111 us  [exchange(): pl.pallas_call(exchange_kernel, out_shape=(pltpu.VMEM((RUNS, 2, 2, TILE,...]
where the time goes in v6:
time: 118 us
  Pallas kernels  116 us (98%)
  between operations  1.45 us (1%)
    pallas_call x1, Pallas kernels, exchange(): pl.pallas_call(exchange_kernel, out_shape=(pltpu.VMEM((RUNS, 2, 2, TILE,...  111 us
    pallas_call x1, Pallas kernels, finish(): pl.pallas_call(finish_kernel, out_shape=(jax.ShapeDtypeStruct(work.shape,...  4.72 us

profile of v6, /device:TPU:20, one launch (start us, length us, event | category | flops | bytes accessed | tf_op | source)
XLA Modules:
  0.0 117.6 jit_solution(14676889553989085816)
XLA Ops:
  1.3 111.4 %exchange.1 = (bf16[16,2,2,128,128]{4,3,2,1,0:T(8,128)(2,1)S(1)}, bf16[16,2,2,128,128]{4,3,2,1,0:T(8,128)(2,1)S(1)}, bf16[640,256]{1,0:T(8,128)(2,1)S(1)}, f32[640,1280]{1,0:T(8,128)S(1)}, s32[16,4,128]{2,1,0:T(4,128)S(1)}) custom-call(s32[1]{0:T(128)S(6)} %copy.8.size_ref, s32[1,32]{1,0:T(1,128)} %index_ref.1, bf16[1,4,128,1024]{3,2,1,0:T(8,128)(2,1)} %bitcast.1, ...), custom_call_target="tpu_custom_call" | custom-call | tf_op jit(solution)/shard_map/exchange/pallas_call | solution.py:385
  112.7 4.7 %finish.1 = (f32[640,1280]{1,0:T(8,128)}, f32[640,256]{1,0:T(8,128)}) custom-call(s32[16,4,128]{2,1,0:T(4,128)S(1)} %get-tuple-element.7.meta_ref, f32[640,1280]{1,0:T(8,128)S(1)} %get-tuple-element.8.work, bf16[16,2,2,128,128]{4,3,2,1,0:T(8,128)(2,1)S(1)} %get-tuple-element.9.arrived_first, ...), custom_call_target="tpu_custom_call" | custom-call | tf_op jit(solution)/shard_map/finish/pallas_call | solution.py:455
